TPU v7x, 32 devices: a whole 2x2x4 slice. The times are simulated.
32 devices in a mesh: groups: 2 (over y), feat: 4 (over z), rows: 2 (over x), sub: 2 (over core).
Axes of the slice: x: 2, y: 2, z: 4, core: 2. Of those that a mesh axis runs over, the one named last changes fastest.
Arguments:
- acts: bfloat16 [256, 32, 8192], P(('groups', 'rows', 'sub'), None, 'feat'), parts along dimension 0, may hold values from -6 to 6
- out_grads: bfloat16 [256, 32, 8192], P(('groups', 'rows', 'sub'), None, 'feat'), parts along dimension 0, may hold values from -6 to 6
- proj_in: bfloat16 [8192, 128], P('feat'), may hold values from -0.0625 to 0.0625
- proj_out: bfloat16 [8192, 128], P('feat'), may hold values from -0.0625 to 0.0625
- store: float32 [5120, 16384], P(('groups', 'rows', 'sub'), 'feat'), parts along dimension 0, may hold values from -0.0084 to 0.0084
Outputs:
- scores: float32 [256, 2560], P(('groups', 'feat'), ('rows', 'sub')), parts along dimension 0
There are 2 independent parts, one for each index of `groups`. A program takes and returns all parts, laid end to end along the dimension named above; an argument that names none is the same for every part. Nothing has to cross between parts.
All inputs are finite; a program needn't handle non-finite values.
Results may differ from a plain program's by a relative error of at most 0.0003.
Values sent between devices are 32-bit elements; how exact they have to be, the bound alone decides.
A program may use at most 64 MiB of HBM per device.

v0:
```python
import jax
import jax.numpy as jnp
from jax import lax
from jax.sharding import PartitionSpec as P


def score_block(grads_block, store):
    return lax.dot_general(
        grads_block,
        store,
        (((1,), (1,)), ((), ())),
        precision=lax.Precision.HIGHEST,
        preferred_element_type=jnp.float32,
    )


def local(acts, out_grads, proj_in, proj_out, store):
    queries_here = acts.shape[0]
    tokens = acts.shape[1]
    width_here = acts.shape[2]
    rank = proj_in.shape[1]
    in_part = jnp.dot(
        acts.reshape(queries_here * tokens, width_here), proj_in, preferred_element_type=jnp.float32
    )
    out_part = jnp.dot(
        out_grads.reshape(queries_here * tokens, width_here),
        proj_out,
        preferred_element_type=jnp.float32,
    )
    in_owned, out_owned = (
        lax.psum_scatter(
            in_part.reshape(queries_here, tokens, rank), "feat", scatter_dimension=0, tiled=True
        ),
        lax.psum_scatter(
            out_part.reshape(queries_here, tokens, rank), "feat", scatter_dimension=0, tiled=True
        ),
    )
    owned = in_owned.shape[0]
    full_grad = jnp.einsum(
        "qti,qtj->qij", out_owned, in_owned, precision=lax.Precision.HIGHEST
    ).reshape(owned, rank * rank)
    query_grad = lax.all_to_all(full_grad, "feat", split_axis=1, concat_axis=0, tiled=True)
    partial_scores = score_block(
        lax.all_gather(query_grad, ("rows", "sub"), axis=0, tiled=True), store
    )
    scores = lax.psum_scatter(partial_scores, "feat", scatter_dimension=0, tiled=True)
    return scores


def solution(mesh):
    return jax.shard_map(
        local,
        mesh=mesh,
        in_specs=(
            P(("groups", "rows", "sub"), None, "feat"),
            P(("groups", "rows", "sub"), None, "feat"),
            P("feat", None),
            P("feat", None),
            P(("groups", "rows", "sub"), "feat"),
        ),
        out_specs=P(("groups", "feat"), ("rows", "sub")),
        check_vma=False,
    )
```

profile of v0, /device:TPU:0, one launch (start us, length us, event | category | flops | bytes accessed | tf_op | source)
XLA Modules:
  0.0 142.3 jit_solution(16457488728892822400)
XLA Ops:
  6.5 0.0 copy-start
  6.5 0.0 copy-start.1
  6.5 0.0 reduce-scatter.6.cloned.1.call-start
  6.5 1.0 copy-done
  7.6 4.2 %fusion = f32[32,32,128]{2,1,0:T(8,128)} fusion(bf16[32,32,2048]{2,1,0:T(8,128)(2,1)} %param.5, bf16[2048,128]{1,0:T(8,128)(2,1)S(1)} %copy-done), kind=kOutput, calls=%fused_computation | convolution fusion | flops 536870912 | bytes 5242880 | tf_op jit(solution)/shard_map/dot_general | solution.py:22
  11.8 0.0 reduce-scatter.6.cloned.1.call-update
  11.8 0.0 reduce-scatter.4.cloned.1.call-start
  11.9 0.0 copy-done.1
  11.9 4.2 %fusion.2 = f32[32,32,128]{2,1,0:T(8,128)} fusion(bf16[32,32,2048]{2,1,0:T(8,128)(2,1)} %param.6, bf16[2048,128]{1,0:T(8,128)(2,1)S(1)} %copy-done.1), kind=kOutput, calls=%fused_computation.2 | convolution fusion | flops 536870912 | bytes 5242880 | tf_op jit(solution)/shard_map/dot_general | solution.py:25
  16.1 0.0 reduce-scatter.4.cloned.1.call-update
  16.1 0.0 all-gather.2.cloned.1.call-start
  16.2 20.4 %reduce-scatter.6.cloned.1.call-done = f32[8,32,128]{2,1,0:T(8,128)} async-done(((f32[32,32,128]{2,1,0:T(8,128)}), f32[8,32,128]{2,1,0:T(8,128)}) %reduce-scatter.6.cloned.1.call-update) | async-done | bytes 131088 | tf_op jit(solution)/shard_map/reduce_scatter | solution.py:31
  36.5 22.4 %reduce-scatter.4.cloned.1.call-done = f32[8,32,128]{2,1,0:T(8,128)} async-done(((f32[32,32,128]{2,1,0:T(8,128)}), f32[8,32,128]{2,1,0:T(8,128)}) %reduce-scatter.4.cloned.1.call-update) | async-done | bytes 131088 | tf_op jit(solution)/shard_map/reduce_scatter | solution.py:34
  59.0 2.0 %fusion.4 = f32[8,128,128]{2,1,0:T(8,128)S(1)} fusion(f32[8,32,128]{2,1,0:T(8,128)} %reduce-scatter.4.cloned.1.call-done, f32[8,32,128]{2,1,0:T(8,128)} %reduce-scatter.6.cloned.1.call-done), kind=kOutput, calls=%fused_computation.4 | convolution fusion | flops 50331648 | bytes 786432 | tf_op jit(solution)/shard_map/qti,qtj->qij/dot_general | solution.py:39
  61.0 0.2 all_to_all.14
  61.1 0.3 copy.6
  61.5 16.3 %all_to_all.19 = f32[8,4,4096]{2,0,1:T(8,128)} all-to-all(f32[8,4,4096]{2,0,1:T(8,128)S(1)} %copy.6), channel_id=1, replica_groups=mesh['groups'=2,'feat'=4,'rows'=2,'sub'=2] {'feat'}, dimensions={1} | all-to-all | bytes 1048576 | tf_op jit(solution)/shard_map/all_to_all | solution.py:42
  77.7 0.0 all-gather.2.cloned.1.call-update
  77.8 0.2 reduce-scatter.8.cloned.1.call-start
  78.0 21.5 %all-gather.2.cloned.1.call-done = f32[128,4096]{1,0:T(8,128)} async-done(((f32[32,4096]{1,0:T(8,128)}), f32[128,4096]{1,0:T(8,128)}) %all-gather.2.cloned.1.call-update) | async-done | bytes 2097168 | tf_op jit(solution)/shard_map/all_gather | solution.py:44
  99.5 15.5 %fusion.5 = f32[128,640]{1,0:T(8,128)} fusion(f32[128,4096]{1,0:T(8,128)} %all-gather.2.cloned.1.call-done, f32[640,4096]{1,0:T(8,128)} %param.9), kind=kOutput, calls=%fused_computation.5 | convolution fusion | flops 4026531840 | bytes 12910592 | tf_op jit(solution)/shard_map/dot_general | solution.py:8
  115.0 0.0 reduce-scatter.8.cloned.1.call-update
  115.0 20.7 %reduce-scatter.8.cloned.1.call-done = f32[32,640]{1,0:T(8,128)} async-done(((f32[128,640]{1,0:T(8,128)}), f32[32,640]{1,0:T(8,128)}) %reduce-scatter.8.cloned.1.call-update) | async-done | bytes 81936 | tf_op jit(solution)/shard_map/reduce_scatter | solution.py:46
Async XLA Ops:
  6.5 1.0 copy-start
  6.5 5.3 %copy-start.1 = (bf16[2048,128]{1,0:T(8,128)(2,1)S(1)}, bf16[2048,128]{1,0:T(8,128)(2,1)}, u32[]{:S(2)}) copy-start(bf16[2048,128]{1,0:T(8,128)(2,1)} %param.8) | copy-start | bytes 1572868
  6.5 30.0 %reduce-scatter.6.cloned.1.call-start = ((), (), s32[]{:S(2)}) async-start(), calls=%async_computation.5 | async-start | bytes 655360 | tf_op jit(solution)/shard_map/reduce_scatter | solution.py:31
  11.8 47.2 %reduce-scatter.4.cloned.1.call-start = ((), (), s32[]{:S(2)}) async-start(), calls=%async_computation.4 | async-start | bytes 655360 | tf_op jit(solution)/shard_map/reduce_scatter | solution.py:34
  16.1 83.4 %all-gather.2.cloned.1.call-start = ((), (), s32[]{:S(2)}) async-start(), calls=%async_computation.6 | async-start | bytes 2621440 | tf_op jit(solution)/shard_map/all_gather | solution.py:44
  77.8 58.0 %reduce-scatter.8.cloned.1.call-start = ((), (), s32[]{:S(2)}) async-start(), calls=%async_computation.7 | async-start | bytes 409600 | tf_op jit(solution)/shard_map/reduce_scatter | solution.py:46
Sparse Core Ops, SparseCore 0:
  11.9 24.5 reduce-scatter.5
  38.8 20.1 reduce-scatter.3
  77.9 21.5 all-gather.1
  115.2 20.5 reduce-scatter.7
where the time goes:
time: 143 us; the launch traced here: 142 us
  waiting for transfers between devices  85 us (59%)
  matrix products  25.9 us (18%)
  blocking collectives  16.3 us (11%)
  between operations  13.2 us (9%)
  local copies, waits for them, and re-layouts  1.53 us (1%)
    reduce_scatter x1, waiting for transfers between devices, local(): lax.psum_scatter(out_part.reshape(queries_here, tokens, rank), 'feat', sc...  22.4 us
    all_gather x1, waiting for transfers between devices, local(): lax.all_gather(query_grad, ('rows', 'sub'), axis=0, tiled=True)  21.5 us
    reduce_scatter x1, waiting for transfers between devices, local(): lax.psum_scatter(partial_scores, 'feat', scatter_dimension=0, tiled=True)  20.7 us
    reduce_scatter x1, waiting for transfers between devices, local(): lax.psum_scatter(in_part.reshape(queries_here, tokens, rank), 'feat', sca...  20.4 us
    all_to_all x1, blocking collectives, local(): lax.all_to_all(full_grad, 'feat', split_axis=1, concat_axis=0, tiled=True)  16.3 us
    dot_general x1, matrix products, score_block(): lax.dot_general(grads_block, store, (((1,), (1,)), ((), ())), precision=l...  15.5 us
    dot_general x1, matrix products, local(): jnp.dot(out_grads.reshape(queries_here * tokens, width_here), proj_out, p...  4.23 us
    dot_general x1, matrix products, local(): jnp.dot(acts.reshape(queries_here * tokens, width_here), proj_in, preferr...  4.22 us
  transfers between devices with their start and end apart: 4, of which 4 were waited for; matrix products, arithmetic and copies ran while one was open for 3% of the time, Pallas kernels for 0%

commit v1 on v0

v1 whole, which is shorter than its diff:
```python
import functools

import jax
import jax.numpy as jnp
from jax import lax
from jax.experimental import pallas as pl
from jax.experimental.pallas import tpu as pltpu
from jax.sharding import PartitionSpec as P

MESH = pl.DeviceIdType.MESH
LANES = 128
F32 = jnp.float32
BF16 = jnp.bfloat16
LAG = 2


def split(x):
    hi = x.astype(BF16)
    return hi, (x - hi.astype(F32)).astype(BF16)


def dot_nt(a, b):
    return lax.dot_general(a, b, (((1,), (1,)), ((), ())), preferred_element_type=F32)


def kernel(
    n, rows, subs, tokens,
    acts, grads, pin, pout, store, out,
    xa, xg, st, shi, slo, own, ups, upr, dns, dnr, tsum, gbuf, glhs, sbuf, rbuf,
    load_sem, z_send, z_recv, x_send, x_recv, c_send, c_recv, f_send, f_recv, s_send, s_recv,
):
    f = lax.axis_index("feat")
    row = lax.axis_index("rows")
    sub = lax.axis_index("sub")
    chunks, tok, _ = xa.shape
    rank = pin.shape[1]
    shard = rank // n
    per = tok // tokens
    here = chunks * per
    total = here * rows * subs
    piece = store.shape[0] // chunks
    mine = total // n
    blocks = sbuf.shape[0]

    def load(kind, c):
        src, dst, size = ((acts, xa, tok), (grads, xg, tok), (store, st, piece))[kind]
        return pltpu.make_async_copy(
            src.at[pl.ds(pl.multiple_of(c * size, size), size)], dst.at[c], load_sem.at[kind, c]
        )

    for c in range(chunks):
        load(0, c).start()
        load(1, c).start()
    for c in range(chunks):
        load(2, c).start()

    barrier = pltpu.get_barrier_semaphore()
    for o in range(1, n):
        pl.semaphore_signal(barrier, device_id={"feat": lax.rem(f + o, n)}, device_id_type=MESH)
    for o in range(1, rows):
        pl.semaphore_signal(barrier, device_id={"rows": lax.rem(row + o, rows)}, device_id_type=MESH)
    for o in range(1, subs):
        pl.semaphore_signal(barrier, device_id={"sub": lax.rem(sub + o, subs)}, device_id_type=MESH)
    pl.semaphore_wait(barrier, n + rows + subs - 3)

    def up(c):
        return pltpu.make_async_remote_copy(
            ups.at[c], upr.at[c], z_send.at[0, c], z_recv.at[0, c],
            device_id={"feat": lax.rem(f + 1, n)}, device_id_type=MESH)

    def down(c):
        return pltpu.make_async_remote_copy(
            dns.at[c], dnr.at[c], z_send.at[1, c], z_recv.at[1, c],
            device_id={"feat": lax.rem(f + n - 1, n)}, device_id_type=MESH)

    def slot(r, s, c):
        size = per * shard
        return gbuf.at[pl.ds(pl.multiple_of(((r * subs + s) * chunks + c) * size, size), size)]

    def across(o, c):
        ref = slot(row, sub, c)
        return pltpu.make_async_remote_copy(
            ref, ref, x_send.at[o - 1, c], x_recv.at[o - 1, c],
            device_id={"rows": lax.rem(row + o, rows)}, device_id_type=MESH)

    def beside(o, c):
        ref = slot(row, sub, c)
        return pltpu.make_async_remote_copy(
            ref, ref, c_send.at[o - 1, c], c_recv.at[o - 1, c],
            device_id={"sub": lax.rem(sub + o, subs)}, device_id_type=MESH)

    def onward(o, p, c):
        ref = slot(lax.rem(row + rows - o, rows), sub, c)
        k = (o - 1) * (subs - 1) + p - 1
        return pltpu.make_async_remote_copy(
            ref, ref, f_send.at[k, c], f_recv.at[k, c],
            device_id={"sub": lax.rem(sub + p, subs)}, device_id_type=MESH)

    def step(s, carry):
        @pl.when(s < chunks)
        def _():
            load(0, s).wait()
            load(1, s).wait()
            a = jnp.dot(xa[s], pin[...], preferred_element_type=F32)
            b = jnp.dot(xg[s], pout[...], preferred_element_type=F32)
            own[s, pl.ds(0, rank), :] = b.T
            own[s, pl.ds(rank, tok), :] = a

        cu = s - f

        @pl.when((cu >= 0) & (cu < chunks))
        def _():
            @pl.when(f > 0)
            def _():
                up(cu).wait_recv()

            @pl.when((f > 0) & (f < n - 1))
            def _():
                ups[cu] = own[cu] + upr[cu]

            @pl.when(f == 0)
            def _():
                ups[cu] = own[cu]

            @pl.when(f < n - 1)
            def _():
                up(cu).start()

        cd = s - (n - 1 - f)

        @pl.when((cd >= 0) & (cd < chunks))
        def _():
            @pl.when(f < n - 1)
            def _():
                down(cd).wait_recv()

            @pl.when((f > 0) & (f < n - 1))
            def _():
                dns[cd] = own[cd] + dnr[cd]

            @pl.when(f == n - 1)
            def _():
                dns[cd] = own[cd]

            @pl.when(f > 0)
            def _():
                down(cd).start()

        c = s - jnp.maximum(f, n - 1 - f)

        @pl.when((c >= 0) & (c < chunks))
        def _():
            tsum[...] = own[c]

            @pl.when(f > 0)
            def _():
                tsum[...] += upr[c]

            @pl.when(f < n - 1)
            def _():
                tsum[...] += dnr[c]

            full_in = tsum[pl.ds(rank, tok), :]
            full_out = tsum[pl.ds(pl.multiple_of(f * shard, shard), shard), :]
            lane = lax.broadcasted_iota(jnp.int32, (shard, tok), 1) // tokens
            wide = jnp.concatenate(
                [jnp.where(lane == q, full_out, 0.0) for q in range(per)], axis=0
            )
            g = lax.dot_general(
                wide, full_in, (((1,), (0,)), ((), ())),
                precision=lax.Precision.HIGHEST, preferred_element_type=F32,
            )
            slot(row, sub, c)[...] = g
            for o in range(1, rows):
                across(o, c).start()
            for o in range(1, subs):
                beside(o, c).start()

        late = c - LAG

        @pl.when((late >= 0) & (late < chunks))
        def _():
            for o in range(1, rows):
                across(o, late).wait_recv()
                for p in range(1, subs):
                    onward(o, p, late).start()

        part = s - LAG

        @pl.when((part >= 0) & (part < chunks))
        def _():
            load(2, part).wait()
            hi, lo = split(st[part])
            at = pl.ds(pl.multiple_of(part * piece, piece), piece)
            shi[at, :] = hi
            slo[at, :] = lo

        return carry

    lax.fori_loop(0, chunks + n - 1 + LAG, step, 0)

    def settle(c, carry):
        @pl.when(f < n - 1)
        def _():
            up(c).wait_send()

        @pl.when(f > 0)
        def _():
            down(c).wait_send()

        for o in range(1, rows):
            across(o, c).wait_send()
        for o in range(1, subs):
            beside(o, c).wait()
        for o in range(1, rows):
            for p in range(1, subs):
                onward(o, p, c).wait()
        return carry

    lax.fori_loop(0, chunks, settle, 0)

    def arrange(r, carry):
        for i in range(shard):
            x = gbuf[pl.ds(r * here * shard + i, here, stride=shard), :]
            hi, lo = split(x)
            at = pl.multiple_of(r * here, here)
            glhs[pl.ds(at, here), pl.ds(i * rank, rank)] = hi
            glhs[pl.ds(total + at, here), pl.ds(i * rank, rank)] = lo
        return carry

    lax.fori_loop(0, rows * subs, arrange, 0)

    def send_scores(o, b):
        peer = lax.rem(f + o, n)
        return pltpu.make_async_remote_copy(
            sbuf.at[b, pl.ds(pl.multiple_of(peer * mine, mine), mine)], rbuf.at[o - 1, b],
            s_send.at[o - 1, b], s_recv.at[o - 1, b],
            device_id={"feat": peer}, device_id_type=MESH)

    def score(b, carry):
        at = pl.ds(pl.multiple_of(b * LANES, LANES), LANES)
        both = dot_nt(glhs[...], shi[at, :])
        cross = dot_nt(glhs[pl.ds(0, total), :], slo[at, :])
        sbuf[b] = both[:total] + (both[total:] + cross)
        for o in range(1, n):
            send_scores(o, b).start()
        return carry

    lax.fori_loop(0, blocks, score, 0)

    for b in range(blocks):
        acc = sbuf[b, pl.ds(pl.multiple_of(f * mine, mine), mine), :]
        for o in range(1, n):
            send_scores(o, b).wait_recv()
            acc = acc + rbuf[o - 1, b]
        out[:, pl.ds(b * LANES, LANES)] = acc
    for b in range(blocks):
        for o in range(1, n):
            send_scores(o, b).wait_send()


def local(n, rows, subs, acts, out_grads, proj_in, proj_out, store):
    queries, tokens, width = acts.shape
    rank = proj_in.shape[1]
    examples, feats = store.shape
    tok = LANES
    chunks = queries * tokens // tok
    shard = rank // n
    total = queries * rows * subs
    mine = total // n
    blocks = examples // LANES
    dma = pltpu.SemaphoreType.DMA
    line = pltpu.VMEM((chunks, rank + tok, rank), F32)
    vmem = pl.BlockSpec(memory_space=pltpu.VMEM)
    hbm = pl.BlockSpec(memory_space=pl.ANY)
    hops = (rows - 1) * (subs - 1)
    return pl.pallas_call(
        functools.partial(kernel, n, rows, subs, tokens),
        out_shape=jax.ShapeDtypeStruct((mine, examples), F32),
        in_specs=[hbm, hbm, vmem, vmem, hbm],
        out_specs=vmem,
        scratch_shapes=[
            pltpu.VMEM((chunks, tok, width), BF16),
            pltpu.VMEM((chunks, tok, width), BF16),
            pltpu.VMEM((chunks, examples // chunks, feats), F32),
            pltpu.VMEM((examples, feats), BF16),
            pltpu.VMEM((examples, feats), BF16),
            line, line, line, line, line,
            pltpu.VMEM((rank + tok, rank), F32),
            pltpu.VMEM((total * shard, rank), F32),
            pltpu.VMEM((2 * total, feats), BF16),
            pltpu.VMEM((blocks, total, LANES), F32),
            pltpu.VMEM((n - 1, blocks, mine, LANES), F32),
            dma((3, chunks)),
            dma((2, chunks)), dma((2, chunks)),
            dma((rows - 1, chunks)), dma((rows - 1, chunks)),
            dma((subs - 1, chunks)), dma((subs - 1, chunks)),
            dma((hops, chunks)), dma((hops, chunks)),
            dma((n - 1, blocks)), dma((n - 1, blocks)),
        ],
        compiler_params=pltpu.CompilerParams(
            collective_id=0, has_side_effects=True, vmem_limit_bytes=62 << 20
        ),
    )(
        acts.reshape(queries * tokens, width),
        out_grads.reshape(queries * tokens, width),
        proj_in, proj_out, store,
    )


def solution(mesh):
    n, rows, subs = (mesh.shape[a] for a in ("feat", "rows", "sub"))
    return jax.shard_map(
        functools.partial(local, n, rows, subs),
        mesh=mesh,
        in_specs=(
            P(("groups", "rows", "sub"), None, "feat"),
            P(("groups", "rows", "sub"), None, "feat"),
            P("feat", None),
            P("feat", None),
            P(("groups", "rows", "sub"), "feat"),
        ),
        out_specs=P(("groups", "feat"), ("rows", "sub")),
        check_vma=False,
    )
```

time: 143 us -> 67.3 us (0.47)
  waiting for transfers between devices: 85 us -> 0 us
  Pallas kernels: 0 us -> 65.6 us
  matrix products: 25.9 us -> 0 us
  blocking collectives: 16.3 us -> 0 us
  between operations: 13.2 us -> 0.01 us
    pallas_call x0 -> x1, Pallas kernels: none -> 65.6 us  [local(): pl.pallas_call(functools.partial(kernel, n, rows, subs, tokens), out_shap...]
    reduce_scatter x3 -> x0, waiting for transfers between devices: 63.5 us -> none  [the longest x1 22.4 us: local(): lax.psum_scatter(out_part.reshape(queries_here, tokens, rank), 'feat', sc...]
    dot_general x4 -> x0, matrix products: 25.9 us -> none  [the longest x1 15.5 us: score_block(): lax.dot_general(grads_block, store, (((1,), (1,)), ((), ())), precision=l...]
    all_gather x1 -> x0, waiting for transfers between devices: 21.5 us -> none  [local(): lax.all_gather(query_grad, ('rows', 'sub'), axis=0, tiled=True)]
    all_to_all x1 -> x0, blocking collectives: 16.3 us -> none  [local(): lax.all_to_all(full_grad, 'feat', split_axis=1, concat_axis=0, tiled=True)]
  transfers between devices with their start and end apart: 4 -> 0, of which waited for: 4 -> 0; matrix products, arithmetic and copies ran while one was open for 3% -> 0% of each run, Pallas kernels for 0% -> 0%
where the time goes in v1:
time: 67.3 us; the launch traced here: 67.1 us
  Pallas kernels  65.6 us (97%)
  local copies, waits for them, and re-layouts  1.53 us (2%)
    pallas_call x1, Pallas kernels, local(): pl.pallas_call(functools.partial(kernel, n, rows, subs, tokens), out_shap...  65.6 us
    unnamed x1, local copies, waits for them, and re-layouts  1.53 us

profile of v1, /device:TPU:0, one launch (start us, length us, event | category | flops | bytes accessed | tf_op | source)
XLA Modules:
  0.0 67.1 jit_solution(16255986005531438955)
XLA Ops:
  0.0 65.6 %shard_map.55 = f32[32,640]{1,0:T(8,128)} custom-call(bf16[1024,2048]{1,0:T(8,128)(2,1)} %bitcast.2, bf16[1024,2048]{1,0:T(8,128)(2,1)} %bitcast.3, bf16[2048,128]{1,0:T(8,128)(2,1)} %pin.1, bf16[2048,128]{1,0:T(8,128)(2,1)} %pout.1, f32[640,4096]{1,0:T(8,128)} %store.1), custom_call_target="tpu_custom_call" | custom-call | tf_op jit(solution)/shard_map/pallas_call | solution.py:277
  65.6 1.5 %copy.7 = f32[32,640]{1,0:T(8,128)} copy(f32[32,640]{1,0:T(8,128)} %shard_map.55) | data formatting | bytes 163840

commit v2 on v1

--- a/solution.py
+++ b/solution.py
@@ -12,6 +12,7 @@
 F32 = jnp.float32
 BF16 = jnp.bfloat16
 LAG = 2
+SKEW = 2
 
 
 def split(x):
@@ -63,14 +64,16 @@
         pl.semaphore_signal(barrier, device_id={"sub": lax.rem(sub + o, subs)}, device_id_type=MESH)
     pl.semaphore_wait(barrier, n + rows + subs - 3)
 
-    def up(c):
-        return pltpu.make_async_remote_copy(
-            ups.at[c], upr.at[c], z_send.at[0, c], z_recv.at[0, c],
+    def up(k, c):
+        at = pl.ds((k + 1) * shard, rank + tok - (k + 1) * shard)
+        return pltpu.make_async_remote_copy(
+            ups.at[c, at], upr.at[c, at], z_send.at[0, c], z_recv.at[0, c],
             device_id={"feat": lax.rem(f + 1, n)}, device_id_type=MESH)
 
-    def down(c):
-        return pltpu.make_async_remote_copy(
-            dns.at[c], dnr.at[c], z_send.at[1, c], z_recv.at[1, c],
+    def down(k, c):
+        at = pl.ds(0, tok + k * shard)
+        return pltpu.make_async_remote_copy(
+            dns.at[c, at], dnr.at[c, at], z_send.at[1, c], z_recv.at[1, c],
             device_id={"feat": lax.rem(f + n - 1, n)}, device_id_type=MESH)
 
     def slot(r, s, c):
@@ -103,65 +106,62 @@
             load(1, s).wait()
             a = jnp.dot(xa[s], pin[...], preferred_element_type=F32)
             b = jnp.dot(xg[s], pout[...], preferred_element_type=F32)
-            own[s, pl.ds(0, rank), :] = b.T
+            bt = b.T
+            own[s, pl.ds(0, rank), :] = bt
             own[s, pl.ds(rank, tok), :] = a
-
-        cu = s - f
+            own[s, pl.ds(rank + tok, rank), :] = bt
+
+        cu = s - SKEW * f
 
         @pl.when((cu >= 0) & (cu < chunks))
         def _():
+            for k in range(n):
+                @pl.when(f == k)
+                def _():
+                    if k > 0:
+                        up(k - 1, cu).wait_recv()
+                    if k < n - 1:
+                        at = pl.ds((k + 1) * shard, rank + tok - (k + 1) * shard)
+                        x = own[cu, at, :]
+                        ups[cu, at, :] = x + upr[cu, at, :] if k > 0 else x
+                        up(k, cu).start()
+
+        cd = s - SKEW * (n - 1 - f)
+
+        @pl.when((cd >= 0) & (cd < chunks))
+        def _():
+            for k in range(n):
+                @pl.when(f == k)
+                def _():
+                    if k < n - 1:
+                        down(k + 1, cd).wait_recv()
+                    if k > 0:
+                        at = pl.ds(0, tok + k * shard)
+                        x = own[cd, pl.ds(rank, tok + k * shard), :]
+                        dns[cd, at, :] = x + dnr[cd, at, :] if k < n - 1 else x
+                        down(k, cd).start()
+
+        c = s - SKEW * jnp.maximum(f, n - 1 - f)
+
+        @pl.when((c >= 0) & (c < chunks))
+        def _():
+            low = pl.ds(pl.multiple_of(f * shard, shard), shard)
+            high = pl.ds(pl.multiple_of(tok + f * shard, shard), shard)
+            tsum[pl.ds(0, tok), :] = own[c, pl.ds(rank, tok), :]
+            tsum[pl.ds(tok, shard), :] = own[c, low, :]
+
             @pl.when(f > 0)
             def _():
-                up(cu).wait_recv()
-
-            @pl.when((f > 0) & (f < n - 1))
-            def _():
-                ups[cu] = own[cu] + upr[cu]
-
-            @pl.when(f == 0)
-            def _():
-                ups[cu] = own[cu]
+                tsum[pl.ds(0, tok), :] += upr[c, pl.ds(rank, tok), :]
+                tsum[pl.ds(tok, shard), :] += upr[c, low, :]
 
             @pl.when(f < n - 1)
             def _():
-                up(cu).start()
-
-        cd = s - (n - 1 - f)
-
-        @pl.when((cd >= 0) & (cd < chunks))
-        def _():
-            @pl.when(f < n - 1)
-            def _():
-                down(cd).wait_recv()
-
-            @pl.when((f > 0) & (f < n - 1))
-            def _():
-                dns[cd] = own[cd] + dnr[cd]
-
-            @pl.when(f == n - 1)
-            def _():
-                dns[cd] = own[cd]
-
-            @pl.when(f > 0)
-            def _():
-                down(cd).start()
-
-        c = s - jnp.maximum(f, n - 1 - f)
-
-        @pl.when((c >= 0) & (c < chunks))
-        def _():
-            tsum[...] = own[c]
-
-            @pl.when(f > 0)
-            def _():
-                tsum[...] += upr[c]
-
-            @pl.when(f < n - 1)
-            def _():
-                tsum[...] += dnr[c]
-
-            full_in = tsum[pl.ds(rank, tok), :]
-            full_out = tsum[pl.ds(pl.multiple_of(f * shard, shard), shard), :]
+                tsum[pl.ds(0, tok), :] += dnr[c, pl.ds(0, tok), :]
+                tsum[pl.ds(tok, shard), :] += dnr[c, high, :]
+
+            full_in = tsum[pl.ds(0, tok), :]
+            full_out = tsum[pl.ds(tok, shard), :]
             lane = lax.broadcasted_iota(jnp.int32, (shard, tok), 1) // tokens
             wide = jnp.concatenate(
                 [jnp.where(lane == q, full_out, 0.0) for q in range(per)], axis=0
@@ -197,16 +197,16 @@
 
         return carry
 
-    lax.fori_loop(0, chunks + n - 1 + LAG, step, 0)
+    lax.fori_loop(0, chunks + SKEW * (n - 1) + LAG, step, 0)
 
     def settle(c, carry):
-        @pl.when(f < n - 1)
-        def _():
-            up(c).wait_send()
-
-        @pl.when(f > 0)
-        def _():
-            down(c).wait_send()
+        for k in range(n):
+            @pl.when(f == k)
+            def _():
+                if k < n - 1:
+                    up(k, c).wait_send()
+                if k > 0:
+                    down(k, c).wait_send()
 
         for o in range(1, rows):
             across(o, c).wait_send()
@@ -285,8 +285,9 @@
             pltpu.VMEM((chunks, examples // chunks, feats), F32),
             pltpu.VMEM((examples, feats), BF16),
             pltpu.VMEM((examples, feats), BF16),
-            line, line, line, line, line,
-            pltpu.VMEM((rank + tok, rank), F32),
+            pltpu.VMEM((chunks, 2 * rank + tok, rank), F32),
+            line, line, line, line,
+            pltpu.VMEM((tok + shard, rank), F32),
             pltpu.VMEM((total * shard, rank), F32),
             pltpu.VMEM((2 * total, feats), BF16),
             pltpu.VMEM((blocks, total, LANES), F32),

time: 67.3 us -> 53.9 us (0.80)
  Pallas kernels: 65.6 us -> 52.2 us
    pallas_call x1, Pallas kernels: 65.6 us -> 52.2 us  [local(): pl.pallas_call(functools.partial(kernel, n, rows, subs, tokens), out_shap...]
where the time goes in v2:
time: 53.9 us; the launch traced here: 53.8 us
  Pallas kernels  52.2 us (97%)
  local copies, waits for them, and re-layouts  1.53 us (3%)
    pallas_call x1, Pallas kernels, local(): pl.pallas_call(functools.partial(kernel, n, rows, subs, tokens), out_shap...  52.2 us
    unnamed x1, local copies, waits for them, and re-layouts  1.53 us

profile of v2, /device:TPU:0, one launch (start us, length us, event | category | flops | bytes accessed | tf_op | source)
XLA Modules:
  0.0 53.8 jit_solution(8612300044871372911)
XLA Ops:
  0.0 52.2 %shard_map.55 = f32[32,640]{1,0:T(8,128)} custom-call(bf16[1024,2048]{1,0:T(8,128)(2,1)} %bitcast.2, bf16[1024,2048]{1,0:T(8,128)(2,1)} %bitcast.3, bf16[2048,128]{1,0:T(8,128)(2,1)} %pin.1, bf16[2048,128]{1,0:T(8,128)(2,1)} %pout.1, f32[640,4096]{1,0:T(8,128)} %store.1), custom_call_target="tpu_custom_call" | custom-call | tf_op jit(solution)/shard_map/pallas_call | solution.py:277
  52.2 1.5 %copy.7 = f32[32,640]{1,0:T(8,128)} copy(f32[32,640]{1,0:T(8,128)} %shard_map.55) | data formatting | bytes 163840

commit v3 on v2

--- a/solution.py
+++ b/solution.py
@@ -12,6 +12,8 @@
 F32 = jnp.float32
 BF16 = jnp.bfloat16
 LAG = 2
+AHEAD = 2
+HOLD = 2
 SKEW = 2
 
 
@@ -26,9 +28,10 @@
 
 def kernel(
     n, rows, subs, tokens,
-    acts, grads, pin, pout, store, out,
+    acts, grads, pin_hbm, pout_hbm, store, out,
+    pin, pout,
     xa, xg, st, shi, slo, own, ups, upr, dns, dnr, tsum, gbuf, glhs, sbuf, rbuf,
-    load_sem, z_send, z_recv, x_send, x_recv, c_send, c_recv, f_send, f_recv, s_send, s_recv,
+    proj_sem, load_sem, z_send, z_recv, x_send, x_recv, c_send, c_recv, f_send, f_recv, s_send, s_recv,
 ):
     f = lax.axis_index("feat")
     row = lax.axis_index("rows")
@@ -49,11 +52,16 @@
             src.at[pl.ds(pl.multiple_of(c * size, size), size)], dst.at[c], load_sem.at[kind, c]
         )
 
-    for c in range(chunks):
+    proj = (
+        pltpu.make_async_copy(pin_hbm, pin, proj_sem.at[0]),
+        pltpu.make_async_copy(pout_hbm, pout, proj_sem.at[1]),
+    )
+    for kind in range(2):
+        proj[kind].start()
+        load(kind, 0).start()
+    for c in range(1, min(AHEAD, chunks)):
         load(0, c).start()
         load(1, c).start()
-    for c in range(chunks):
-        load(2, c).start()
 
     barrier = pltpu.get_barrier_semaphore()
     for o in range(1, n):
@@ -100,6 +108,20 @@
             device_id={"sub": lax.rem(sub + p, subs)}, device_id_type=MESH)
 
     def step(s, carry):
+        @pl.when(s == 0)
+        def _():
+            proj[0].wait()
+            proj[1].wait()
+
+        @pl.when(s + AHEAD < chunks)
+        def _():
+            load(0, s + AHEAD).start()
+            load(1, s + AHEAD).start()
+
+        @pl.when((s >= HOLD) & (s < HOLD + chunks))
+        def _():
+            load(2, s - HOLD).start()
+
         @pl.when(s < chunks)
         def _():
             load(0, s).wait()
@@ -185,7 +207,7 @@
                 for p in range(1, subs):
                     onward(o, p, late).start()
 
-        part = s - LAG
+        part = s - HOLD - LAG
 
         @pl.when((part >= 0) & (part < chunks))
         def _():
@@ -277,9 +299,11 @@
     return pl.pallas_call(
         functools.partial(kernel, n, rows, subs, tokens),
         out_shape=jax.ShapeDtypeStruct((mine, examples), F32),
-        in_specs=[hbm, hbm, vmem, vmem, hbm],
+        in_specs=[hbm, hbm, hbm, hbm, hbm],
         out_specs=vmem,
         scratch_shapes=[
+            pltpu.VMEM(proj_in.shape, BF16),
+            pltpu.VMEM(proj_out.shape, BF16),
             pltpu.VMEM((chunks, tok, width), BF16),
             pltpu.VMEM((chunks, tok, width), BF16),
             pltpu.VMEM((chunks, examples // chunks, feats), F32),
@@ -292,7 +316,7 @@
             pltpu.VMEM((2 * total, feats), BF16),
             pltpu.VMEM((blocks, total, LANES), F32),
             pltpu.VMEM((n - 1, blocks, mine, LANES), F32),
-            dma((3, chunks)),
+            dma((2,)), dma((3, chunks)),
             dma((2, chunks)), dma((2, chunks)),
             dma((rows - 1, chunks)), dma((rows - 1, chunks)),
             dma((subs - 1, chunks)), dma((subs - 1, chunks)),

time: 53.9 us -> 52.8 us (0.980)
  Pallas kernels: 52.2 us -> 51.1 us
    pallas_call x1, Pallas kernels: 52.2 us -> 51.1 us  [local(): pl.pallas_call(functools.partial(kernel, n, rows, subs, tokens), out_shap...]
where the time goes in v3:
time: 52.8 us; the launch traced here: 52.6 us
  Pallas kernels  51.1 us (97%)
  local copies, waits for them, and re-layouts  1.53 us (3%)
    pallas_call x1, Pallas kernels, local(): pl.pallas_call(functools.partial(kernel, n, rows, subs, tokens), out_shap...  51.1 us
    unnamed x1, local copies, waits for them, and re-layouts  1.53 us

profile of v3, /device:TPU:0, one launch (start us, length us, event | category | flops | bytes accessed | tf_op | source)
XLA Modules:
  0.0 52.6 jit_solution(728882084052408969)
XLA Ops:
  0.0 51.1 %shard_map.55 = f32[32,640]{1,0:T(8,128)} custom-call(bf16[1024,2048]{1,0:T(8,128)(2,1)} %bitcast.2, bf16[1024,2048]{1,0:T(8,128)(2,1)} %bitcast.3, bf16[2048,128]{1,0:T(8,128)(2,1)} %pin_hbm.1, bf16[2048,128]{1,0:T(8,128)(2,1)} %pout_hbm.1, f32[640,4096]{1,0:T(8,128)} %store.1), custom_call_target="tpu_custom_call" | custom-call | tf_op jit(solution)/shard_map/pallas_call | solution.py:299
  51.1 1.5 %copy.7 = f32[32,640]{1,0:T(8,128)} copy(f32[32,640]{1,0:T(8,128)} %shard_map.55) | data formatting | bytes 163840

commit v4 on v3

--- a/solution.py
+++ b/solution.py
@@ -9,6 +9,7 @@
 
 MESH = pl.DeviceIdType.MESH
 LANES = 128
+WIDE = 384
 F32 = jnp.float32
 BF16 = jnp.bfloat16
 LAG = 2
@@ -44,7 +45,8 @@
     total = here * rows * subs
     piece = store.shape[0] // chunks
     mine = total // n
-    blocks = sbuf.shape[0]
+    examples = store.shape[0]
+    blocks = [(e, min(WIDE, examples - e)) for e in range(0, examples, WIDE)]
 
     def load(kind, c):
         src, dst, size = ((acts, xa, tok), (grads, xg, tok), (store, st, piece))[kind]
@@ -254,29 +256,29 @@
 
     def send_scores(o, b):
         peer = lax.rem(f + o, n)
-        return pltpu.make_async_remote_copy(
-            sbuf.at[b, pl.ds(pl.multiple_of(peer * mine, mine), mine)], rbuf.at[o - 1, b],
+        cols = pl.ds(*blocks[b])
+        return pltpu.make_async_remote_copy(
+            sbuf.at[pl.ds(pl.multiple_of(peer * mine, mine), mine), cols],
+            rbuf.at[o - 1, pl.ds(0, mine), cols],
             s_send.at[o - 1, b], s_recv.at[o - 1, b],
             device_id={"feat": peer}, device_id_type=MESH)
 
-    def score(b, carry):
-        at = pl.ds(pl.multiple_of(b * LANES, LANES), LANES)
+    for b in range(len(blocks)):
+        at = pl.ds(*blocks[b])
         both = dot_nt(glhs[...], shi[at, :])
         cross = dot_nt(glhs[pl.ds(0, total), :], slo[at, :])
-        sbuf[b] = both[:total] + (both[total:] + cross)
+        sbuf[:, at] = both[:total] + (both[total:] + cross)
         for o in range(1, n):
             send_scores(o, b).start()
-        return carry
-
-    lax.fori_loop(0, blocks, score, 0)
-
-    for b in range(blocks):
-        acc = sbuf[b, pl.ds(pl.multiple_of(f * mine, mine), mine), :]
+
+    for b in range(len(blocks)):
+        cols = pl.ds(*blocks[b])
+        acc = sbuf[pl.ds(pl.multiple_of(f * mine, mine), mine), cols]
         for o in range(1, n):
             send_scores(o, b).wait_recv()
-            acc = acc + rbuf[o - 1, b]
-        out[:, pl.ds(b * LANES, LANES)] = acc
-    for b in range(blocks):
+            acc = acc + rbuf[o - 1, :, cols]
+        out[:, cols] = acc
+    for b in range(len(blocks)):
         for o in range(1, n):
             send_scores(o, b).wait_send()
 
@@ -290,7 +292,7 @@
     shard = rank // n
     total = queries * rows * subs
     mine = total // n
-    blocks = examples // LANES
+    blocks = pl.cdiv(examples, WIDE)
     dma = pltpu.SemaphoreType.DMA
     line = pltpu.VMEM((chunks, rank + tok, rank), F32)
     vmem = pl.BlockSpec(memory_space=pltpu.VMEM)
@@ -314,8 +316,8 @@
             pltpu.VMEM((tok + shard, rank), F32),
             pltpu.VMEM((total * shard, rank), F32),
             pltpu.VMEM((2 * total, feats), BF16),
-            pltpu.VMEM((blocks, total, LANES), F32),
-            pltpu.VMEM((n - 1, blocks, mine, LANES), F32),
+            pltpu.VMEM((total, examples), F32),
+            pltpu.VMEM((n - 1, mine, examples), F32),
             dma((2,)), dma((3, chunks)),
             dma((2, chunks)), dma((2, chunks)),
             dma((rows - 1, chunks)), dma((rows - 1, chunks)),

time: 52.8 us -> 54.2 us (1.027)
  Pallas kernels: 51.1 us -> 52.5 us
    pallas_call x1, Pallas kernels: 51.1 us -> 52.5 us  [local(): pl.pallas_call(functools.partial(kernel, n, rows, subs, tokens), out_shap...]
where the time goes in v4:
time: 54.2 us; the launch traced here: 54 us
  Pallas kernels  52.5 us (97%)
  local copies, waits for them, and re-layouts  1.53 us (3%)
    pallas_call x1, Pallas kernels, local(): pl.pallas_call(functools.partial(kernel, n, rows, subs, tokens), out_shap...  52.5 us
    unnamed x1, local copies, waits for them, and re-layouts  1.53 us

profile of v4, /device:TPU:0, one launch (start us, length us, event | category | flops | bytes accessed | tf_op | source)
XLA Modules:
  0.0 54.0 jit_solution(14817337302639703682)
XLA Ops:
  0.0 52.5 %shard_map.55 = f32[32,640]{1,0:T(8,128)} custom-call(bf16[1024,2048]{1,0:T(8,128)(2,1)} %bitcast.2, bf16[1024,2048]{1,0:T(8,128)(2,1)} %bitcast.3, bf16[2048,128]{1,0:T(8,128)(2,1)} %pin_hbm.1, bf16[2048,128]{1,0:T(8,128)(2,1)} %pout_hbm.1, f32[640,4096]{1,0:T(8,128)} %store.1), custom_call_target="tpu_custom_call" | custom-call | tf_op jit(solution)/shard_map/pallas_call | solution.py:301
  52.5 1.5 %copy.7 = f32[32,640]{1,0:T(8,128)} copy(f32[32,640]{1,0:T(8,128)} %shard_map.55) | data formatting | bytes 163840
